TPU v7x, 256 devices: a whole 4x4x8 slice. The times are simulated.
256 devices in a mesh: row: 16 (over x, y), col: 16 (over z, core).
Axes of the slice: x: 4, y: 4, z: 8, core: 2. Of those that a mesh axis runs over, the one named last changes fastest.
Arguments:
- start_block: float32 [65536, 128], P(('row', 'col')), may hold values from -6 to 6
- vertex_scale: float32 [65536], P(('row', 'col')), may hold values from 0.015625 to 0.0625
- adj_tiles: bfloat16 [16, 16, 64, 128, 128], P('row', 'col'), may hold values from 0 to 1
- tile_row: int32 [16, 16, 64], P('row', 'col'), may hold values from 0 to 31
- tile_col: int32 [16, 16, 64], P('row', 'col'), may hold values from 0 to 31
- live_count: int32 [16, 16], P('row', 'col'), may hold values from 16 to 64, as said below
- rotation_first: float32 [256, 128], replicated, may hold values from -0.375 to 0.375
- rotation_second: float32 [384, 128], replicated, may hold values from -0.3125 to 0.3125
Outputs:
- final_block: float32 [65536, 128], P(('row', 'col'))
- final_image: float32 [65536, 128], P(('row', 'col'))
Inputs may be any that keep to these rules, and one draw needn't show every extreme that they name: Slots from live_count on are ignored; at least one device has all 64 slots live in every draw.
All inputs are finite; a program needn't handle non-finite values.
Results may differ from a plain program's by a relative error of at most 0.01.
Values may be sent and summed in bfloat16 or wider, within the bound.
A program may use at most 64 MiB of HBM per device.

v0:
```python
import jax
import jax.numpy as jnp
from jax import lax
from jax.sharding import PartitionSpec as P

HIGH = lax.Precision.HIGHEST


def tile_products(tiles_here, cols_here, count_here, flat_panel, span_slots, tile_side, width_k):
    alive_mask = jnp.arange(span_slots, dtype=jnp.int32) < count_here
    pieces = jnp.take(flat_panel, cols_here, axis=0)
    pieces = jnp.where(alive_mask[:, None], pieces, jnp.zeros_like(pieces))
    pieces = pieces.reshape(span_slots, tile_side, width_k)
    tile_out = jnp.einsum("tab,tbk->tak", tiles_here, pieces, preferred_element_type=jnp.float32)
    return tile_out.reshape(span_slots, tile_side * width_k)


def place_rows(rows_slot, tile_out, row_tiles, tile_side, width_k):
    placed = jax.ops.segment_sum(tile_out, rows_slot, num_segments=row_tiles)
    return placed.reshape(row_tiles * tile_side, width_k)


def apply_operator(block, vertex_scale, tiles_here, rows_here, cols_here, count_here):
    tile_side = tiles_here.shape[-1]
    width_k = block.shape[1]
    slot_total = tiles_here.shape[0]
    scaled = (vertex_scale[:, None] * block).astype(jnp.bfloat16)
    gathered = lax.all_gather(scaled, "col", axis=0, tiled=True)
    flat_panel = gathered.reshape(gathered.shape[0] // tile_side, tile_side * width_k)
    row_tiles = lax.axis_size("row") * block.shape[0] // tile_side
    tile_out = tile_products(
        tiles_here, cols_here, count_here, flat_panel, slot_total, tile_side, width_k
    )
    partial_value = place_rows(rows_here, tile_out, row_tiles, tile_side, width_k)
    summed = lax.psum_scatter(
        partial_value.astype(jnp.bfloat16), "row", scatter_dimension=0, tiled=True
    ).astype(jnp.float32)
    return block - vertex_scale[:, None] * summed


def inner(left, right):
    return jnp.einsum("sk,sl->kl", left, right, precision=HIGH)


def residual_block(block, image, verts_all):
    gram = lax.psum(inner(block, image), ("row", "col")) / verts_all
    resid = image - jnp.dot(block, gram, precision=HIGH)
    colsq = lax.psum(jnp.sum(resid * resid, axis=0), ("row", "col"))
    return resid * lax.rsqrt(colsq / verts_all + 1e-06)


def local(
    start_block,
    vertex_scale,
    adj_tiles,
    tile_row,
    tile_col,
    live_count,
    rotation_first,
    rotation_second,
):
    width_k = start_block.shape[1]
    verts_all = start_block.shape[0] * lax.axis_size("row") * lax.axis_size("col")
    tiles_here = adj_tiles[0, 0]
    rows_here = tile_row[0, 0]
    cols_here = tile_col[0, 0]
    count_here = live_count[0, 0]

    def oper(block):
        return apply_operator(block, vertex_scale, tiles_here, rows_here, cols_here, count_here)

    image0 = oper(start_block)
    search0 = residual_block(start_block, image0, verts_all)
    simage0 = oper(search0)
    rot_x, rot_w = (rotation_first[:width_k], rotation_first[width_k:])
    block1 = jnp.dot(start_block, rot_x, precision=HIGH) + jnp.dot(search0, rot_w, precision=HIGH)
    image1 = jnp.dot(image0, rot_x, precision=HIGH) + jnp.dot(simage0, rot_w, precision=HIGH)
    prev1 = jnp.dot(search0, rot_w, precision=HIGH)
    pimage1 = jnp.dot(simage0, rot_w, precision=HIGH)
    search1 = residual_block(block1, image1, verts_all)
    simage1 = oper(search1)
    rot_qx = rotation_second[:width_k]
    rot_qw = rotation_second[width_k : 2 * width_k]
    rot_qp = rotation_second[2 * width_k :]
    final_block = (
        jnp.dot(block1, rot_qx, precision=HIGH)
        + jnp.dot(search1, rot_qw, precision=HIGH)
        + jnp.dot(prev1, rot_qp, precision=HIGH)
    )
    final_image = (
        jnp.dot(image1, rot_qx, precision=HIGH)
        + jnp.dot(simage1, rot_qw, precision=HIGH)
        + jnp.dot(pimage1, rot_qp, precision=HIGH)
    )
    return (final_block, final_image)


def solution(mesh):
    placed = (
        P(("row", "col"), None),
        P(("row", "col")),
        P("row", "col", None, None, None),
        P("row", "col", None),
        P("row", "col", None),
        P("row", "col"),
        P(),
        P(),
    )
    return jax.shard_map(
        local,
        mesh=mesh,
        in_specs=placed,
        out_specs=(P(("row", "col"), None), P(("row", "col"), None)),
        check_vma=False,
    )
```

profile of v0, /device:TPU:2, one launch (start us, length us, event | category | flops | bytes accessed | tf_op | source)
XLA Modules:
  0.0 1100.4 jit_solution(16218495195349804594)
XLA Ops:
  7.2 1.1 copy.23
  8.4 1.3 multiply_convert_fusion.2
  10.4 0.7 compare_select_fusion
  11.1 0.7 compare_and_fusion
  11.7 39.2 %all-gather.4.cloned.1.call-done = bf16[4096,128]{0,1:T(8,128)(2,1)} async-done(((bf16[256,128]{0,1:T(8,128)(2,1)}), bf16[4096,128]{0,1:T(8,128)(2,1)}) %all-gather.4.cloned.1.call-update) | async-done | bytes 1048592 | tf_op jit(solution)/shard_map/all_gather | solution.py:28
  51.0 2.3 copy.19
  53.2 1.5 reshape.49
  54.8 3.2 gather_fusion
  58.0 1.9 fusion.14
  59.9 0.6 copy.40
  60.5 3.6 convolution_bitcast_fusion.2
  64.0 5.6 copy.21
  69.6 10.6 scatter_custom_fusion
  80.3 1.7 convert_element_type.37
  82.0 1.3 convert_element_type.38
  83.3 2.3 copy.22
  85.6 76.8 %reduce-scatter.4.cloned.1.call-done = bf16[256,128]{0,1:T(8,128)(2,1)} async-done(((bf16[4096,128]{0,1:T(8,128)(2,1)}), bf16[256,128]{0,1:T(8,128)(2,1)}) %reduce-scatter.4.cloned.1.call-update) | async-done | bytes 65552 | tf_op jit(solution)/shard_map/reduce_scatter | solution.py:35
  162.4 1.7 convolution_bitcast_fusion.4
  164.3 241.9 %all-reduce.3.cloned.1.call-done = f32[128,128]{0,1:T(8,128)} async-done(((f32[128,128]{0,1:T(8,128)}), f32[128,128]{0,1:T(8,128)}) %all-reduce.3.cloned.1.call-update) | async-done | bytes 65552 | tf_op jit(solution)/shard_map/psum | solution.py:46
  406.2 1.2 multiply_reduce_fusion.1
  407.4 74.2 %psum.29 = f32[128]{0:T(128)S(1)} all-reduce(f32[128]{0:T(128)S(1)} %get-tuple-element.3), channel_id=1, replica_groups=mesh['row'=16,'col'=16] {'row','col'}, use_global_device_ids=true, to_apply=%region_4.6 | all-reduce | flops 128 | bytes 1024 | tf_op jit(solution)/shard_map/psum | solution.py:48
  481.6 0.5 copy-done.12
  482.1 0.7 multiply_convert_fusion.1
  483.1 33.3 %all-gather.6.cloned.1.call-done = bf16[4096,128]{0,1:T(8,128)(2,1)} async-done(((bf16[256,128]{0,1:T(8,128)(2,1)}), bf16[4096,128]{0,1:T(8,128)(2,1)}) %all-gather.6.cloned.1.call-update) | async-done | bytes 1048592 | tf_op jit(solution)/shard_map/all_gather | solution.py:28
  516.4 2.3 copy.24
  518.7 1.5 reshape.52
  520.2 3.2 gather_fusion.1
  523.4 1.9 fusion.13
  525.3 0.6 copy.42
  525.9 3.6 convolution_bitcast_fusion.1
  529.5 5.6 copy.26
  535.1 10.6 scatter_custom_fusion.1
  545.7 1.7 convert_element_type.41
  547.4 1.3 convert_element_type.42
  548.7 2.3 copy.27
  551.3 0.5 fusion.29
  552.1 75.8 %reduce-scatter.6.cloned.1.call-done = bf16[256,128]{0,1:T(8,128)(2,1)} async-done(((bf16[4096,128]{0,1:T(8,128)(2,1)}), bf16[256,128]{0,1:T(8,128)(2,1)}) %reduce-scatter.6.cloned.1.call-update) | async-done | bytes 65552 | tf_op jit(solution)/shard_map/reduce_scatter | solution.py:35
  627.9 1.3 fusion.22
  629.2 0.6 copy-done.6
  629.9 0.3 convolution_add_fusion.4
  630.3 0.9 fusion.55
  631.2 238.6 %all-reduce.5.cloned.1.call-done = f32[128,128]{0,1:T(8,128)} async-done(((f32[128,128]{0,1:T(8,128)}), f32[128,128]{0,1:T(8,128)}) %all-reduce.5.cloned.1.call-update) | async-done | bytes 65552 | tf_op jit(solution)/shard_map/psum | solution.py:46
  869.8 1.2 multiply_reduce_fusion
  871.0 74.2 %psum.31 = f32[128]{0:T(128)S(1)} all-reduce(f32[128]{0:T(128)S(1)} %get-tuple-element.5), channel_id=1, replica_groups=mesh['row'=16,'col'=16] {'row','col'}, use_global_device_ids=true, to_apply=%region_9.11 | all-reduce | flops 128 | bytes 1024 | tf_op jit(solution)/shard_map/psum | solution.py:48
  945.2 0.7 multiply_convert_fusion
  946.0 33.5 %all-gather.8.cloned.1.call-done = bf16[4096,128]{0,1:T(8,128)(2,1)} async-done(((bf16[256,128]{0,1:T(8,128)(2,1)}), bf16[4096,128]{0,1:T(8,128)(2,1)}) %all-gather.8.cloned.1.call-update) | async-done | bytes 1048592 | tf_op jit(solution)/shard_map/all_gather | solution.py:28
  979.5 2.3 copy.31
  981.8 1.5 reshape.55
  983.3 3.2 gather_fusion.2
  986.5 1.9 fusion.12
  988.4 0.6 copy.44
  989.0 3.6 convolution_bitcast_fusion
  992.6 5.6 copy.33
  998.2 10.6 scatter_custom_fusion.2
  1008.8 1.7 convert_element_type.45
  1010.5 1.3 convert_element_type.46
  1011.8 2.3 copy.34
  1014.1 0.3 fusion.45
  1014.4 0.4 fusion.43
  1014.8 0.5 convolution_add_fusion.3
  1015.3 0.9 convolution_add_fusion.2
  1016.2 74.7 %reduce-scatter.8.cloned.1.call-done = bf16[256,128]{0,1:T(8,128)(2,1)} async-done(((bf16[4096,128]{0,1:T(8,128)(2,1)}), bf16[256,128]{0,1:T(8,128)(2,1)}) %reduce-scatter.8.cloned.1.call-update) | async-done | bytes 65552 | tf_op jit(solution)/shard_map/reduce_scatter | solution.py:35
  1090.9 1.3 convolution_add_fusion.1
  1092.2 0.9 convolution_add_fusion
  (47 shorter events, 1.3 us)
Async XLA Ops:
  7.2 53.3 %copy-start = (bf16[1,1,64,128,128]{4,3,2,1,0:T(8,128)(2,1)S(1)}, bf16[1,1,64,128,128]{4,3,2,1,0:T(8,128)(2,1)}, u32[]{:S(2)}) copy-start(bf16[1,1,64,128,128]{4,3,2,1,0:T(8,128)(2,1)} %param.12) | copy-start | bytes 6291460
  7.2 43.8 %all-gather.4.cloned.1.call-start = ((), (), s32[]{:S(2)}) async-start(), calls=%async_computation.3 | async-start | bytes 1114112 | tf_op jit(solution)/shard_map/all_gather | solution.py:28
  9.7 152.7 %reduce-scatter.4.cloned.1.call-start = ((), (), s32[]{:S(2)}) async-start(), calls=%async_computation.4 | async-start | bytes 1114112 | tf_op jit(solution)/shard_map/reduce_scatter | solution.py:35
  83.3 79.2 %copy-start.1 = (f32[256,128]{1,0:T(8,128)S(1)}, f32[256,128]{1,0:T(8,128)}, u32[]{:S(2)}) copy-start(f32[256,128]{1,0:T(8,128)} %param.10) | copy-start | bytes 393220
  83.3 79.2 %copy-start.11 = (f32[256]{0:T(256)S(1)}, f32[256]{0:T(256)}, u32[]{:S(2)}) copy-start(f32[256]{0:T(256)} %param.11) | copy-start | bytes 3076
  85.6 320.6 %all-reduce.3.cloned.1.call-start = ((), (), s32[]{:S(2)}) async-start(), calls=%async_computation.5 | async-start | bytes 131072 | tf_op jit(solution)/shard_map/psum | solution.py:46
  164.2 352.2 %all-gather.6.cloned.1.call-start = ((), (), s32[]{:S(2)}) async-start(), calls=%async_computation.6 | async-start | bytes 1114112 | tf_op jit(solution)/shard_map/all_gather | solution.py:28
  481.6 0.5 copy-start.12
  482.9 145.0 %reduce-scatter.6.cloned.1.call-start = ((), (), s32[]{:S(2)}) async-start(), calls=%async_computation.7 | async-start | bytes 1114112 | tf_op jit(solution)/shard_map/reduce_scatter | solution.py:35
  548.7 2.6 copy-start.10
  548.7 2.6 copy-start.13
  548.7 81.2 %copy-start.9 = (bf16[256,128]{0,1:T(8,128)(2,1)S(1)}, bf16[256,128]{0,1:T(8,128)(2,1)}, u32[]{:S(2)}) copy-start(bf16[256,128]{0,1:T(8,128)(2,1)} %reduce-scatter.4.cloned.1.call-done) | copy-start | bytes 196612
  551.0 318.8 %all-reduce.5.cloned.1.call-start = ((), (), s32[]{:S(2)}) async-start(), calls=%async_computation.8 | async-start | bytes 131072 | tf_op jit(solution)/shard_map/psum | solution.py:46
  551.8 427.7 %copy-start.4 = (f32[256,128]{1,0:T(8,128)}, f32[256,128]{1,0:T(8,128)S(1)}, u32[]{:S(2)}) copy-start(f32[256,128]{1,0:T(8,128)S(1)} %fusion.29) | copy-start | bytes 393220
  552.1 427.4 %copy-start.2 = (f32[256,128]{1,0:T(8,128)}, f32[256,128]{1,0:T(8,128)S(1)}, u32[]{:S(2)}) copy-start(f32[256,128]{1,0:T(8,128)S(1)} %convolution_add_fusion.5) | copy-start | bytes 393220
  629.2 0.6 copy-start.6
  631.2 348.3 %all-gather.8.cloned.1.call-start = ((), (), s32[]{:S(2)}) async-start(), calls=%async_computation.9 | async-start | bytes 1114112 | tf_op jit(solution)/shard_map/all_gather | solution.py:28
  945.9 145.0 %reduce-scatter.8.cloned.1.call-start = ((), (), s32[]{:S(2)}) async-start(), calls=%async_computation.10 | async-start | bytes 1114112 | tf_op jit(solution)/shard_map/reduce_scatter | solution.py:35
  1011.8 2.3 copy-start.3
  1011.8 2.4 copy-start.8
  1011.8 3.5 copy-start.5
  1014.1 78.1 %copy-start.7 = (f32[256,128]{1,0:T(8,128)S(1)}, f32[256,128]{1,0:T(8,128)}, u32[]{:S(2)}) copy-start(f32[256,128]{1,0:T(8,128)} %copy-done.6) | copy-start | bytes 393220
Sparse Core Ops, SparseCore 0:
  10.3 40.5 all-gather.3
  85.7 76.6 reduce-scatter.3
  169.4 236.6 all-reduce.2
  483.0 33.3 all-gather.5
  551.2 76.6 reduce-scatter.5
  633.3 236.4 all-reduce.4
  946.1 33.3 all-gather.7
  1014.2 76.6 reduce-scatter.7
where the time goes:
time: 1110 us; the launch traced here: 1100 us
  waiting for transfers between devices  814 us (73%)
  blocking collectives  148 us (13%)
  local copies, waits for them, and re-layouts  52.7 us (5%)
  other arithmetic  46.7 us (4%)
  matrix products  22.4 us (2%)
  between operations  15.4 us (1%)
    psum x2, waiting for transfers between devices, residual_block(): gram = lax.psum(inner(block, image), ('row', 'col')) / verts_all  480 us
    reduce_scatter x3, waiting for transfers between devices, apply_operator(): lax.psum_scatter(partial_value.astype(jnp.bfloat16), 'row', scatter_dimen...  227 us
    psum x2, blocking collectives, residual_block(): colsq = lax.psum(jnp.sum(resid * resid, axis=0), ('row', 'col'))  148 us
    all_gather x3, waiting for transfers between devices, apply_operator(): gathered = lax.all_gather(scaled, 'col', axis=0, tiled=True)  106 us
    scatter-add x3, other arithmetic, place_rows(): placed = jax.ops.segment_sum(tile_out, rows_slot, num_segments=row_tiles)  31.9 us
  transfers between devices with their start and end apart: 8, of which 8 were waited for; matrix products, arithmetic and copies ran while one was open for 0% of the time, Pallas kernels for 0%

commit v1 on v0

--- a/solution.py
+++ b/solution.py
@@ -43,7 +43,7 @@
 
 
 def residual_block(block, image, verts_all):
-    gram = lax.psum(inner(block, image), ("row", "col")) / verts_all
+    gram = jnp.sum(lax.all_gather(inner(block, image), ("row", "col")), axis=0) / verts_all
     resid = image - jnp.dot(block, gram, precision=HIGH)
     colsq = lax.psum(jnp.sum(resid * resid, axis=0), ("row", "col"))
     return resid * lax.rsqrt(colsq / verts_all + 1e-06)

time: 1110 us -> 939 us (0.85)
  waiting for transfers between devices: 814 us -> 600 us
  other arithmetic: 46.7 us -> 76 us
  local copies, waits for them, and re-layouts: 52.7 us -> 67.2 us
    psum x2 -> x0, waiting for transfers between devices: 480 us -> none  [residual_block(): gram = lax.psum(inner(block, image), ('row', 'col')) / verts_all]
    all_gather x0 -> x2, waiting for transfers between devices: none -> 264 us  [residual_block(): lax.all_gather(inner(block, image), ('row', 'col'))]
    reduce_sum x0 -> x2, other arithmetic: none -> 14.7 us  [residual_block(): jnp.sum(lax.all_gather(inner(block, image), ('row', 'col')), axis=0)]
    scatter-add x3, other arithmetic: 31.9 us -> 46.5 us  [place_rows(): placed = jax.ops.segment_sum(tile_out, rows_slot, num_segments=row_tiles)]
    unnamed x32 -> x35, local copies, waits for them, and re-layouts: 4.05 us -> 18.2 us
where the time goes in v1:
time: 939 us; the launch traced here: 929 us
  waiting for transfers between devices  600 us (64%)
  blocking collectives  150 us (16%)
  other arithmetic  76 us (8%)
  local copies, waits for them, and re-layouts  67.2 us (7%)
  matrix products  20.8 us (2%)
  between operations  15.5 us (2%)
    all_gather x2, waiting for transfers between devices, residual_block(): lax.all_gather(inner(block, image), ('row', 'col'))  264 us
    reduce_scatter x3, waiting for transfers between devices, apply_operator(): lax.psum_scatter(partial_value.astype(jnp.bfloat16), 'row', scatter_dimen...  228 us
    psum x2, blocking collectives, residual_block(): colsq = lax.psum(jnp.sum(resid * resid, axis=0), ('row', 'col'))  150 us
    all_gather x3, waiting for transfers between devices, apply_operator(): gathered = lax.all_gather(scaled, 'col', axis=0, tiled=True)  108 us
    scatter-add x3, other arithmetic, place_rows(): placed = jax.ops.segment_sum(tile_out, rows_slot, num_segments=row_tiles)  46.5 us
  transfers between devices with their start and end apart: 8, of which 8 were waited for; matrix products, arithmetic and copies ran while one was open for 0% of the time, Pallas kernels for 0%

profile of v1, /device:TPU:2, one launch (start us, length us, event | category | flops | bytes accessed | tf_op | source)
XLA Modules:
  0.0 929.5 jit_solution(4004446786603117345)
XLA Ops:
  7.2 1.1 copy.57
  8.4 1.3 multiply_convert_fusion.2
  10.4 0.7 compare_select_fusion
  11.1 0.7 compare_and_fusion
  11.7 39.2 %all-gather.8.cloned.1.call-done = bf16[4096,128]{0,1:T(8,128)(2,1)} async-done(((bf16[256,128]{0,1:T(8,128)(2,1)}), bf16[4096,128]{0,1:T(8,128)(2,1)}) %all-gather.8.cloned.1.call-update) | async-done | bytes 1048592 | tf_op jit(solution)/shard_map/all_gather | solution.py:28
  51.0 2.3 copy.53
  53.3 1.5 reshape.49
  54.8 3.2 gather_fusion
  58.0 1.9 fusion.14
  59.9 0.6 copy.75
  60.5 3.6 convolution_bitcast_fusion.2
  64.1 5.6 copy.55
  69.7 25.2 %scatter_custom_fusion = f32[32,16384]{1,0:T(8,128)} fusion(s32[64]{0:T(128)} %bitcast.74, f32[8,8,128,128]{3,2,1,0:T(8,128)} %bitcast.69, f32[]{:T(128)} %constant.4.clone.1), kind=kCustom, calls=%fused_computation.13 | custom fusion | flops 1048576 | bytes 6291968 | tf_op jit(solution)/shard_map/scatter-add | solution.py:19
  94.9 1.7 convert_element_type.37
  96.6 1.3 convert_element_type.38
  97.9 2.3 copy.56
  100.3 76.8 %reduce-scatter.4.cloned.1.call-done = bf16[256,128]{0,1:T(8,128)(2,1)} async-done(((bf16[4096,128]{0,1:T(8,128)(2,1)}), bf16[256,128]{0,1:T(8,128)(2,1)}) %reduce-scatter.4.cloned.1.call-update) | async-done | bytes 65552 | tf_op jit(solution)/shard_map/reduce_scatter | solution.py:35
  177.1 1.7 convolution_bitcast_fusion.4
  178.9 139.2 %all-gather.14.cloned.1.call-done = f32[32768,128]{0,1:T(8,128)} async-done(((f32[128,128]{0,1:T(8,128)}), f32[32768,128]{0,1:T(8,128)}) %all-gather.14.cloned.1.call-update) | async-done | bytes 16777232 | tf_op jit(solution)/shard_map/all_gather | solution.py:46
  318.1 14.1 %copy.77 = f32[16,8,256,128]{3,2,1,0:T(8,128)} copy(f32[16,8,256,128]{3,1,2,0:T(8,128)} %bitcast.67) | data formatting | bytes 33554432
  332.2 8.1 bitcast_reduce_fusion
  340.3 0.4 multiply_reduce_fusion.1
  340.7 75.4 %psum.14 = f32[128]{0:T(128)S(1)} all-reduce(f32[128]{0:T(128)S(1)} %get-tuple-element.3), channel_id=1, replica_groups=mesh['row'=16,'col'=16] {'row','col'}, use_global_device_ids=true, to_apply=%region_4.6 | all-reduce | flops 128 | bytes 1024 | tf_op jit(solution)/shard_map/psum | solution.py:48
  416.1 0.5 copy-done.13
  416.6 0.7 multiply_convert_fusion.1
  417.4 34.4 %all-gather.10.cloned.1.call-done = bf16[4096,128]{0,1:T(8,128)(2,1)} async-done(((bf16[256,128]{0,1:T(8,128)(2,1)}), bf16[4096,128]{0,1:T(8,128)(2,1)}) %all-gather.10.cloned.1.call-update) | async-done | bytes 1048592 | tf_op jit(solution)/shard_map/all_gather | solution.py:28
  451.8 2.3 copy.58
  454.1 1.5 reshape.52
  455.6 3.2 gather_fusion.1
  458.8 1.9 fusion.13
  460.7 0.6 copy.78
  461.3 3.6 convolution_bitcast_fusion.1
  464.9 5.6 copy.60
  470.5 10.6 %scatter_custom_fusion.1 = f32[32,16384]{1,0:T(8,128)} fusion(s32[64]{0:T(128)} %bitcast.75, f32[8,8,128,128]{3,2,1,0:T(8,128)} %bitcast.70, f32[]{:T(128)} %constant.4.clone.1), kind=kCustom, calls=%fused_computation.10 | custom fusion | flops 1048576 | bytes 6291968 | tf_op jit(solution)/shard_map/scatter-add | solution.py:19
  481.1 1.7 convert_element_type.41
  482.8 1.3 convert_element_type.42
  484.1 2.3 copy.61
  486.6 0.5 fusion.29
  487.3 76.0 %reduce-scatter.6.cloned.1.call-done = bf16[256,128]{0,1:T(8,128)(2,1)} async-done(((bf16[4096,128]{0,1:T(8,128)(2,1)}), bf16[256,128]{0,1:T(8,128)(2,1)}) %reduce-scatter.6.cloned.1.call-update) | async-done | bytes 65552 | tf_op jit(solution)/shard_map/reduce_scatter | solution.py:35
  563.4 1.3 fusion.22
  564.7 0.7 copy-done.6
  565.8 1.0 fusion.55
  566.8 124.8 %all-gather.16.cloned.1.call-done = f32[32768,128]{1,0:T(8,128)} async-done(((f32[128,128]{1,0:T(8,128)}), f32[32768,128]{1,0:T(8,128)}) %all-gather.16.cloned.1.call-update) | async-done | bytes 16777232 | tf_op jit(solution)/shard_map/all_gather | solution.py:46
  691.6 6.6 reduce_sum.38
  698.7 74.6 %psum.15 = f32[128]{0:T(128)S(1)} all-reduce(f32[128]{0:T(128)S(1)} %get-tuple-element.5), channel_id=1, replica_groups=mesh['row'=16,'col'=16] {'row','col'}, use_global_device_ids=true, to_apply=%region_9.11 | all-reduce | flops 128 | bytes 1024 | tf_op jit(solution)/shard_map/psum | solution.py:48
  773.3 0.7 multiply_convert_fusion
  774.3 34.2 %all-gather.12.cloned.1.call-done = bf16[4096,128]{0,1:T(8,128)(2,1)} async-done(((bf16[256,128]{0,1:T(8,128)(2,1)}), bf16[4096,128]{0,1:T(8,128)(2,1)}) %all-gather.12.cloned.1.call-update) | async-done | bytes 1048592 | tf_op jit(solution)/shard_map/all_gather | solution.py:28
  808.5 2.3 copy.66
  810.7 1.5 reshape.55
  812.3 3.2 gather_fusion.2
  815.5 1.9 fusion.12
  817.4 0.6 copy.80
  818.0 3.6 convolution_bitcast_fusion
  821.6 5.6 copy.68
  827.2 10.6 %scatter_custom_fusion.2 = f32[32,16384]{1,0:T(8,128)} fusion(s32[64]{0:T(128)} %bitcast.76, f32[8,8,128,128]{3,2,1,0:T(8,128)} %bitcast.68, f32[]{:T(128)} %constant.4.clone.1), kind=kCustom, calls=%fused_computation.7 | custom fusion | flops 1048576 | bytes 6291968 | tf_op jit(solution)/shard_map/scatter-add | solution.py:19
  837.8 1.7 convert_element_type.45
  839.5 1.3 convert_element_type.46
  840.8 2.3 copy.69
  843.5 0.4 fusion.43
  843.9 0.5 convolution_add_fusion.3
  844.3 0.9 convolution_add_fusion.2
  845.2 74.8 %reduce-scatter.8.cloned.1.call-done = bf16[256,128]{0,1:T(8,128)(2,1)} async-done(((bf16[4096,128]{0,1:T(8,128)(2,1)}), bf16[256,128]{0,1:T(8,128)(2,1)}) %reduce-scatter.8.cloned.1.call-update) | async-done | bytes 65552 | tf_op jit(solution)/shard_map/reduce_scatter | solution.py:35
  920.0 1.3 convolution_add_fusion.1
  921.3 0.9 convolution_add_fusion
  (53 shorter events, 2.1 us)
Async XLA Ops:
  7.2 53.3 %copy-start = (bf16[1,1,64,128,128]{4,3,2,1,0:T(8,128)(2,1)S(1)}, bf16[1,1,64,128,128]{4,3,2,1,0:T(8,128)(2,1)}, u32[]{:S(2)}) copy-start(bf16[1,1,64,128,128]{4,3,2,1,0:T(8,128)(2,1)} %param.12) | copy-start | bytes 6291460
  7.2 43.8 %all-gather.8.cloned.1.call-start = ((), (), s32[]{:S(2)}) async-start(), calls=%async_computation.3 | async-start | bytes 1114112 | tf_op jit(solution)/shard_map/all_gather | solution.py:28
  9.7 167.4 %reduce-scatter.4.cloned.1.call-start = ((), (), s32[]{:S(2)}) async-start(), calls=%async_computation.4 | async-start | bytes 1114112 | tf_op jit(solution)/shard_map/reduce_scatter | solution.py:35
  97.9 79.2 %copy-start.1 = (f32[256,128]{1,0:T(8,128)S(1)}, f32[256,128]{1,0:T(8,128)}, u32[]{:S(2)}) copy-start(f32[256,128]{1,0:T(8,128)} %param.10) | copy-start | bytes 393220
  97.9 79.2 %copy-start.12 = (f32[256]{0:T(256)S(1)}, f32[256]{0:T(256)}, u32[]{:S(2)}) copy-start(f32[256]{0:T(256)} %param.11) | copy-start | bytes 3076
  100.3 217.8 %all-gather.14.cloned.1.call-start = ((), (), s32[]{:S(2)}) async-start(), calls=%async_computation.9 | async-start | bytes 16842752 | tf_op jit(solution)/shard_map/all_gather | solution.py:46
  178.9 272.9 %all-gather.10.cloned.1.call-start = ((), (), s32[]{:S(2)}) async-start(), calls=%async_computation.5 | async-start | bytes 1114112 | tf_op jit(solution)/shard_map/all_gather | solution.py:28
  332.2 8.1 copy-start.9
  416.1 0.5 copy-start.13
  417.3 146.0 %reduce-scatter.6.cloned.1.call-start = ((), (), s32[]{:S(2)}) async-start(), calls=%async_computation.6 | async-start | bytes 1114112 | tf_op jit(solution)/shard_map/reduce_scatter | solution.py:35
  484.1 2.4 copy-start.11
  484.1 2.4 copy-start.14
  484.1 81.3 %copy-start.10 = (bf16[256,128]{0,1:T(8,128)(2,1)S(1)}, bf16[256,128]{0,1:T(8,128)(2,1)}, u32[]{:S(2)}) copy-start(bf16[256,128]{0,1:T(8,128)(2,1)} %reduce-scatter.4.cloned.1.call-done) | copy-start | bytes 196612
  486.5 205.1 %all-gather.16.cloned.1.call-start = ((), (), s32[]{:S(2)}) async-start(), calls=%async_computation.10 | async-start | bytes 16842752 | tf_op jit(solution)/shard_map/all_gather | solution.py:46
  487.0 211.2 %copy-start.4 = (f32[256,128]{1,0:T(8,128)}, f32[256,128]{1,0:T(8,128)S(1)}, u32[]{:S(2)}) copy-start(f32[256,128]{1,0:T(8,128)S(1)} %fusion.29) | copy-start | bytes 393220
  487.3 211.0 %copy-start.2 = (f32[256,128]{1,0:T(8,128)}, f32[256,128]{1,0:T(8,128)S(1)}, u32[]{:S(2)}) copy-start(f32[256,128]{1,0:T(8,128)S(1)} %convolution_add_fusion.5) | copy-start | bytes 393220
  564.7 0.7 copy-start.6
  566.8 241.7 %all-gather.12.cloned.1.call-start = ((), (), s32[]{:S(2)}) async-start(), calls=%async_computation.7 | async-start | bytes 1114112 | tf_op jit(solution)/shard_map/all_gather | solution.py:28
  774.0 146.0 %reduce-scatter.8.cloned.1.call-start = ((), (), s32[]{:S(2)}) async-start(), calls=%async_computation.8 | async-start | bytes 1114112 | tf_op jit(solution)/shard_map/reduce_scatter | solution.py:35
  840.8 2.4 copy-start.3
  840.8 2.4 copy-start.8
  840.8 3.5 copy-start.5
  843.1 78.2 %copy-start.7 = (f32[256,128]{1,0:T(8,128)S(1)}, f32[256,128]{1,0:T(8,128)}, u32[]{:S(2)}) copy-start(f32[256,128]{1,0:T(8,128)} %copy-done.6) | copy-start | bytes 393220
Sparse Core Ops, SparseCore 0:
  10.3 40.5 all-gather.7
  100.4 76.6 reduce-scatter.3
  182.2 135.9 all-gather.13
  417.5 34.2 all-gather.9
  486.6 76.6 reduce-scatter.5
  566.9 124.6 all-gather.15
  774.2 34.2 all-gather.11
  843.3 76.6 reduce-scatter.7
